TPU v7x, 512 devices: a whole 4x4x16 slice. The times are simulated.
512 devices in a mesh: wide: 64 (over z, x), narrow: 8 (over y, core).
Axes of the slice: x: 4, y: 4, z: 16, core: 2. Of those that a mesh axis runs over, the one named last changes fastest.
Arguments:
- sublevel_symbol_entries: bfloat16 [1024, 4, 4096], P('wide', None, 'narrow'), may hold values from -160 to 160
- prior_symbol_memory: bfloat16 [1024, 4096], P('wide', 'narrow'), may hold values from -6 to 6
- entry_scaling_multiplier: float32 [4096], P('narrow'), may hold values from 0.25 to 1.75
- entry_scaling_offset: float32 [4096], P('narrow'), may hold values from -4 to 4
- learned_blending: float32 [6, 4096], P(None, 'narrow'), may hold values from 0 to 1
- blending_lowering_coefficients: bfloat16 [4096, 160], P('narrow'), may hold values from -0.09375 to 0.09375
- blending_raising_coefficients: bfloat16 [5, 32, 4096], P(None, None, 'narrow'), may hold values from -1 to 1
- fading_lowering_coefficients: bfloat16 [4096, 64], P('narrow'), may hold values from -0.09375 to 0.09375
- fading_raising_coefficients: bfloat16 [64, 4096], P(None, 'wide'), may hold values from -0.75 to 0.75
- learned_fading: float32 [4096], P('wide'), may hold values from -6 to 1
- immediate_item_premium: float32 [4096], P('wide'), may hold values from -3 to 3
- acceptor_projection: bfloat16 [4096, 4096], P('narrow', 'wide'), may hold values from -0.09375 to 0.09375
- lookup_projection: bfloat16 [4096, 4096], P('narrow', 'wide'), may hold values from -0.09375 to 0.09375
- payload_projection: bfloat16 [4096, 4096], P('narrow', 'wide'), may hold values from -0.09375 to 0.09375
- gating_projection: bfloat16 [4096, 4096], P('narrow', 'wide'), may hold values from -0.09375 to 0.09375
- emission_projection: bfloat16 [4096, 4096], P(None, 'wide'), may hold values from -0.09375 to 0.09375
- group_scaling_multiplier: float32 [4096], P('wide'), may hold values from 0.25 to 1.75
- group_scaling_offset: float32 [4096], P('wide'), may hold values from -4 to 4
- dialogue_group_memory: float32 [262144, 1024], P('wide', 'narrow'), may hold values from -6 to 6
Outputs:
- mixing_output: bfloat16 [1024, 4, 4096], P('narrow', None, 'wide')
- final_state: float32 [262144, 1024], P('wide', 'narrow')
All inputs are finite; a program needn't handle non-finite values.
Results may differ from a plain program's by a relative error of at most 0.034.
Values may be sent and summed in bfloat16 or wider, within the bound.
A program may use at most 64 MiB of HBM per device.

v0:
```python
import jax
import jax.numpy as jnp
from jax import lax
from jax.sharding import PartitionSpec as P

CHANNEL_SPAN = 64
FEATURE_EXTENT = 4096


def per_device(
    sublevel_symbol_entries,
    prior_symbol_memory,
    entry_scaling_multiplier,
    entry_scaling_offset,
    learned_blending,
    blending_lowering_coefficients,
    blending_raising_coefficients,
    fading_lowering_coefficients,
    fading_raising_coefficients,
    learned_fading,
    immediate_item_premium,
    acceptor_projection,
    lookup_projection,
    payload_projection,
    gating_projection,
    emission_projection,
    group_scaling_multiplier,
    group_scaling_offset,
    dialogue_group_memory,
):
    rank = blending_raising_coefficients.shape[1]
    narrow_rows = dialogue_group_memory.shape[1]
    local_width = emission_projection.shape[1]
    group_partition = local_width // CHANNEL_SPAN
    sessions, steps, features = sublevel_symbol_entries.shape
    weights = (acceptor_projection, lookup_projection, payload_projection, gating_projection)
    floats = sublevel_symbol_entries.astype(jnp.float32)
    stats = lax.psum(jnp.stack([jnp.sum(floats, -1), jnp.sum(floats * floats, -1)], 0), "narrow")
    center = stats[0][..., None] / FEATURE_EXTENT
    spread = stats[1][..., None] / FEATURE_EXTENT - center * center
    normed = (
        (floats - center) * lax.rsqrt(spread + 1e-05) * entry_scaling_multiplier
        + entry_scaling_offset
    ).astype(jnp.bfloat16)
    previous = jnp.concatenate([prior_symbol_memory[:, None], normed[:, :-1]], 1)
    normalized_float = normed.astype(jnp.float32)
    shifted_input = previous.astype(jnp.float32) - normalized_float
    blended = (normalized_float + shifted_input * learned_blending[0]).astype(jnp.bfloat16)
    partial_mix = jnp.einsum(
        "smd,dr->smr", blended, blending_lowering_coefficients, preferred_element_type=jnp.float32
    )
    hidden_activation = jnp.tanh(lax.psum(partial_mix, "narrow")).astype(jnp.bfloat16)
    decay_shift = jnp.einsum(
        "smr,rd->smd",
        hidden_activation[..., :rank],
        blending_raising_coefficients[0],
        preferred_element_type=jnp.float32,
    )
    decay_mix = (normalized_float + shifted_input * (learned_blending[1] + decay_shift)).astype(
        jnp.bfloat16
    )
    partial_decay = jnp.einsum(
        "smd,dr->smr", decay_mix, fading_lowering_coefficients, preferred_element_type=jnp.float32
    )
    decay_hidden = jnp.tanh(lax.psum(partial_decay, "narrow")).astype(jnp.bfloat16)
    small = jnp.concatenate([hidden_activation[..., rank:], decay_hidden], -1)
    small_width = small.shape[-1]
    packed = jnp.concatenate(
        [prior_symbol_memory]
        + [normed[:, index] for index in range(steps)]
        + [small.reshape(sessions, steps * small_width)],
        -1,
    )
    packed_all = lax.all_gather(
        lax.all_gather(packed, "x", axis=0, tiled=True), "z", axis=0, tiled=True
    )
    small_start = (steps + 1) * features
    term_results = []
    for index in range(steps):
        previous_now = packed_all[:, index * features : (index + 1) * features]
        normed_now = packed_all[:, (index + 1) * features : (index + 2) * features]
        normalized_now = normed_now.astype(jnp.float32)
        shifted_now = previous_now.astype(jnp.float32) - normalized_now
        small_now = small_start + index * small_width
        for selector_index in range(4):
            low_rank_update = jnp.dot(
                packed_all[
                    :, small_now + selector_index * rank : small_now + (selector_index + 1) * rank
                ],
                blending_raising_coefficients[selector_index + 1],
                preferred_element_type=jnp.float32,
            )
            mixed_input = (
                normalized_now
                + shifted_now * (learned_blending[selector_index + 2] + low_rank_update)
            ).astype(jnp.bfloat16)
            term_results.append(
                jnp.dot(
                    mixed_input, weights[selector_index], preferred_element_type=jnp.float32
                ).astype(jnp.bfloat16)
            )
    projected = (
        lax.psum_scatter(
            jnp.concatenate(term_results, -1), "narrow", scatter_dimension=0, tiled=True
        )
        .astype(jnp.float32)
        .reshape(narrow_rows, steps, 4 * local_width)
    )
    rows_start = lax.axis_index("narrow") * narrow_rows
    own_rows = lax.dynamic_slice_in_dim(packed_all[:, small_start:], rows_start, narrow_rows, 0)
    decay_rows = own_rows.reshape(narrow_rows, steps, small_width)[..., 4 * rank :]
    decay_log = learned_fading + jnp.einsum(
        "smr,rd->smd", decay_rows, fading_raising_coefficients, preferred_element_type=jnp.float32
    )
    shrink_coefficient = jnp.exp(-jnp.exp(decay_log))

    def channel_set_first(block):
        return block.reshape(narrow_rows, group_partition, CHANNEL_SPAN).transpose(1, 2, 0)

    state = dialogue_group_memory.reshape(group_partition, CHANNEL_SPAN, CHANNEL_SPAN, narrow_rows)
    reward = immediate_item_premium.reshape(group_partition, CHANNEL_SPAN)
    pieces = []
    for index in range(steps):
        acceptor = channel_set_first(projected[:, index, :local_width])
        key_now = channel_set_first(projected[:, index, local_width : 2 * local_width])
        value_now = channel_set_first(projected[:, index, 2 * local_width : 3 * local_width])
        gate_now = projected[:, index, 3 * local_width :]
        forget_now = channel_set_first(shrink_coefficient[:, index])
        dyadic = key_now[:, :, None, :] * value_now[:, None, :, :]
        retrieval = jnp.sum(
            acceptor[:, :, None, :] * (state + reward[:, :, None, None] * dyadic), 1
        )
        state = forget_now[:, :, None, :] * state + dyadic
        center_r = jnp.mean(retrieval, 1, keepdims=True)
        offset = retrieval - center_r
        scaled = offset * lax.rsqrt(jnp.mean(offset * offset, 1, keepdims=True) + 0.00064)
        squashed = scaled.transpose(2, 0, 1).reshape(narrow_rows, local_width)
        pieces.append(
            (
                (squashed * group_scaling_multiplier + group_scaling_offset) * jax.nn.silu(gate_now)
            ).astype(jnp.bfloat16)
        )
    gated = jnp.stack(pieces, 1).reshape(narrow_rows * steps, local_width).T
    gated_all = lax.all_gather(
        lax.all_gather(gated, "x", axis=0, tiled=True), "z", axis=0, tiled=True
    )
    mixing_output = (
        jnp.einsum("cs,ce->se", gated_all, emission_projection, preferred_element_type=jnp.float32)
        .astype(jnp.bfloat16)
        .reshape(narrow_rows, steps, local_width)
    )
    return (
        mixing_output,
        state.reshape(group_partition * CHANNEL_SPAN * CHANNEL_SPAN, narrow_rows),
    )


def solution(mesh):
    wide_size = mesh.shape["wide"]
    x_size = 4 if wide_size % 4 == 0 else 1
    split = jax.sharding.Mesh(
        mesh.devices.reshape(wide_size // x_size, x_size, mesh.shape["narrow"]),
        ("z", "x", "narrow"),
    )
    wide = ("z", "x")
    placed = (
        P(wide, None, "narrow"),
        P(wide, "narrow"),
        P("narrow"),
        P("narrow"),
        P(None, "narrow"),
        P("narrow", None),
        P(None, None, "narrow"),
        P("narrow", None),
        P(None, wide),
        P(wide),
        P(wide),
        P("narrow", wide),
        P("narrow", wide),
        P("narrow", wide),
        P("narrow", wide),
        P(None, wide),
        P(wide),
        P(wide),
        P(wide, "narrow"),
    )
    return jax.shard_map(
        per_device,
        mesh=split,
        in_specs=placed,
        out_specs=(P("narrow", None, wide), P(wide, "narrow")),
        check_vma=False,
    )
```

profile of v0, /device:TPU:2, one launch (start us, length us, event | category | flops | bytes accessed | tf_op | source)
XLA Modules:
  0.0 373.3 jit_solution(8394787153175697751)
XLA Ops:
  8.3 14.9 %psum.21 = f32[2,16,4]{1,2,0:T(4,128)S(1)} all-reduce(f32[2,16,4]{1,2,0:T(4,128)S(1)} %pad_maximum_fusion.5), channel_id=1, replica_groups=mesh['z'=16,'x'=4,'narrow'=8] {'narrow'}, use_global_device_ids=true, to_apply=%region_2.0 | all-reduce | flops 128 | bytes 1024 | tf_op jit(solution)/shard_map/psum | solution.py:38
  27.0 23.9 %psum.22 = f32[16,4,160]{2,0,1:T(8,128)S(1)} all-reduce(f32[16,4,160]{2,0,1:T(8,128)S(1)} %fusion.180), channel_id=1, replica_groups=mesh['z'=16,'x'=4,'narrow'=8] {'narrow'}, use_global_device_ids=true, to_apply=%region_3.0 | all-reduce | flops 10240 | bytes 81920 | tf_op jit(solution)/shard_map/psum | solution.py:52
  52.2 23.6 %psum.23 = f32[16,4,64]{2,0,1:T(8,128)S(1)} all-reduce(f32[16,4,64]{2,0,1:T(8,128)S(1)} %fusion.98), channel_id=1, replica_groups=mesh['z'=16,'x'=4,'narrow'=8] {'narrow'}, use_global_device_ids=true, to_apply=%region_4.0 | all-reduce | flops 4096 | bytes 32768 | tf_op jit(solution)/shard_map/psum | solution.py:65
  76.0 14.1 %all_gather.12 = bf16[64,3328]{1,0:T(8,128)(2,1)} all-gather(bf16[16,3328]{1,0:T(8,128)(2,1)S(1)} %constant_dynamic-update-slice_fusion), channel_id=1, replica_groups=mesh['z'=16,'x'=4,'narrow'=8] {'x'}, dimensions={0}, use_global_device_ids=true | all-gather | bytes 532480 | tf_op jit(solution)/shard_map/all_gather | solution.py:75
  90.1 91.1 %all-gather.3.cloned.1.call-done = bf16[1024,3328]{1,0:T(8,128)(2,1)} async-done(((bf16[64,3328]{1,0:T(8,128)(2,1)}), bf16[1024,3328]{1,0:T(8,128)(2,1)}) %all-gather.3.cloned.1.call-update) | async-done | bytes 6815760 | tf_op jit(solution)/shard_map/all_gather | solution.py:74
  181.2 2.4 fusion.69
  183.6 2.5 fusion.71
  186.1 2.5 fusion.73
  188.6 2.4 fusion.75
  191.0 2.4 fusion.77
  193.5 2.4 fusion.79
  195.9 2.4 fusion.81
  198.3 2.4 fusion.83
  203.1 2.4 fusion.87
  205.6 2.4 fusion.89
  208.0 2.5 fusion.91
  210.5 2.4 fusion.61
  212.9 2.4 fusion.63
  217.8 2.4 fusion.67
  220.2 2.6 copy.60
  224.7 37.5 %reduce-scatter.4.cloned.1.call-done = bf16[128,1024]{1,0:T(8,128)(2,1)} async-done(((bf16[1024,1024]{1,0:T(8,128)(2,1)}), bf16[128,1024]{1,0:T(8,128)(2,1)}) %reduce-scatter.4.cloned.1.call-update) | async-done | bytes 262160
  272.3 13.0 %all_gather.14 = bf16[256,512]{1,0:T(8,128)(2,1)} all-gather(bf16[64,512]{1,0:T(8,128)(2,1)S(1)} %copy.55), channel_id=1, replica_groups=mesh['z'=16,'x'=4,'narrow'=8] {'x'}, dimensions={0}, use_global_device_ids=true | all-gather | bytes 327680 | tf_op jit(solution)/shard_map/all_gather | solution.py:145
  285.3 77.5 %all-gather.5.cloned.1.call-done = bf16[4096,512]{1,0:T(8,128)(2,1)} async-done(((bf16[256,512]{1,0:T(8,128)(2,1)}), bf16[4096,512]{1,0:T(8,128)(2,1)}) %all-gather.5.cloned.1.call-update) | async-done | bytes 4194320 | tf_op jit(solution)/shard_map/all_gather | solution.py:144
  362.9 3.0 convolution_convert_fusion
  (87 shorter events, 23.8 us)
Async XLA Ops:
  7.2 355.7 %copy-start = (bf16[4096,64]{0,1:T(8,128)(2,1)S(1)}, bf16[4096,64]{0,1:T(8,128)(2,1)}, u32[]{:S(2)}) copy-start(bf16[4096,64]{0,1:T(8,128)(2,1)} %param.34) | copy-start | bytes 1572868
  7.2 174.0 %copy-start.5 = (bf16[5,32,512]{2,1,0:T(8,128)(2,1)S(1)}, bf16[5,32,512]{2,1,0:T(8,128)(2,1)}, u32[]{:S(2)}) copy-start(bf16[5,32,512]{2,1,0:T(8,128)(2,1)} %param.25) | copy-start | bytes 491524
  7.2 174.0 %copy-start.6 = (bf16[512,64]{0,1:T(8,128)(2,1)S(1)}, bf16[512,64]{0,1:T(8,128)(2,1)}, u32[]{:S(2)}) copy-start(bf16[512,64]{0,1:T(8,128)(2,1)} %param.30) | copy-start | bytes 196612
  7.2 174.0 %all-gather.3.cloned.1.call-start = ((), (), s32[]{:S(2)}) async-start(), calls=%async_computation.1 | async-start | bytes 7241728 | tf_op jit(solution)/shard_map/all_gather | solution.py:74
  90.0 93.5 %copy-start.7 = (bf16[512,64]{0,1:T(8,128)(2,1)S(1)}, bf16[512,64]{0,1:T(8,128)(2,1)}, u32[]{:S(2)}) copy-start(bf16[512,64]{0,1:T(8,128)(2,1)} %param.31) | copy-start | bytes 196612
  90.1 172.1 %reduce-scatter.4.cloned.1.call-start = ((), (), s32[]{:S(2)}) async-start(), calls=%async_computation.3 | async-start | bytes 2359296
  183.6 2.5 copy-start.8
  186.1 2.5 copy-start.9
  222.8 0.7 copy-start.2
  222.8 1.4 slice-start
  222.8 1.6 copy-start.10
  222.8 1.6 copy-start.11
  222.8 140.1 %all-gather.5.cloned.1.call-start = ((), (), s32[]{:S(2)}) async-start(), calls=%async_computation.2 | async-start | bytes 4456448 | tf_op jit(solution)/shard_map/all_gather | solution.py:144
  264.0 1.6 copy-start.1
  269.6 2.3 copy-start.3
  269.6 2.3 copy-start.4
Sparse Core Ops, SparseCore 0:
  90.2 90.9 all-gather.2
  222.9 39.2 reduce-scatter.3
  285.5 77.3 all-gather.4
where the time goes:
time: 374 us; the launch traced here: 373 us
  waiting for transfers between devices  206 us (55%)
  blocking collectives  89.5 us (24%)
  matrix products  44.3 us (12%)
  between operations  14.3 us (4%)
  other arithmetic  9.65 us (3%)
  local copies, waits for them, and re-layouts  9.14 us (2%)
    all_gather x1, waiting for transfers between devices, per_device(): lax.all_gather(lax.all_gather(packed, 'x', axis=0, tiled=True), 'z', axis...  91.1 us
    all_gather x1, waiting for transfers between devices, per_device(): lax.all_gather(lax.all_gather(gated, 'x', axis=0, tiled=True), 'z', axis=...  77.5 us
    dot_general x16, matrix products, per_device(): jnp.dot(mixed_input, weights[selector_index], preferred_element_type=jnp....  38.8 us
    unnamed x4, waiting for transfers between devices  37.5 us
    psum x1, blocking collectives, per_device(): lax.psum(partial_mix, 'narrow')  23.9 us
    psum x1, blocking collectives, per_device(): lax.psum(partial_decay, 'narrow')  23.6 us
    psum x1, blocking collectives, per_device(): lax.psum(jnp.stack([jnp.sum(floats, -1), jnp.sum(floats * floats, -1)], 0...  14.9 us
    all_gather x1, blocking collectives, per_device(): lax.all_gather(packed, 'x', axis=0, tiled=True)  14.1 us
  transfers between devices with their start and end apart: 3, of which 3 were waited for; matrix products, arithmetic and copies ran while one was open for 0% of the time, Pallas kernels for 0%

commit v1 on v0

--- a/solution.py
+++ b/solution.py
@@ -142,7 +142,10 @@
         )
     gated = jnp.stack(pieces, 1).reshape(narrow_rows * steps, local_width).T
     gated_all = lax.all_gather(
-        lax.all_gather(gated, "x", axis=0, tiled=True), "z", axis=0, tiled=True
+        jnp.concatenate(lax.all_to_all(jnp.stack([gated] * lax.axis_size("x")), "x", 0, 0), axis=0),
+        "z",
+        axis=0,
+        tiled=True,
     )
     mixing_output = (
         jnp.einsum("cs,ce->se", gated_all, emission_projection, preferred_element_type=jnp.float32)

time: 374 us -> 371 us (level)
  the two profiles are of different devices: /device:TPU:2 before, /device:TPU:4 now
where the time goes in v1:
time: 371 us; the launch traced here: 370 us
  waiting for transfers between devices  206 us (56%)
  blocking collectives  85.8 us (23%)
  matrix products  44.3 us (12%)
  between operations  14.3 us (4%)
  other arithmetic  9.65 us (3%)
  local copies, waits for them, and re-layouts  9.15 us (2%)
    all_gather x1, waiting for transfers between devices, per_device(): lax.all_gather(lax.all_gather(packed, 'x', axis=0, tiled=True), 'z', axis...  90.4 us
    all_gather x1, waiting for transfers between devices, per_device(): lax.all_gather(jnp.concatenate(lax.all_to_all(jnp.stack([gated] * lax.axi...  78.3 us
    dot_general x16, matrix products, per_device(): jnp.dot(mixed_input, weights[selector_index], preferred_element_type=jnp....  38.8 us
    unnamed x4, waiting for transfers between devices  37.5 us
    psum x1, blocking collectives, per_device(): lax.psum(partial_mix, 'narrow')  23.9 us
    psum x1, blocking collectives, per_device(): lax.psum(partial_decay, 'narrow')  23.6 us
    psum x1, blocking collectives, per_device(): lax.psum(jnp.stack([jnp.sum(floats, -1), jnp.sum(floats * floats, -1)], 0...  14.9 us
    all_gather x1, blocking collectives, per_device(): lax.all_gather(packed, 'x', axis=0, tiled=True)  14.7 us
  transfers between devices with their start and end apart: 3, of which 3 were waited for; matrix products, arithmetic and copies ran while one was open for 0% of the time, Pallas kernels for 0%

profile of v1, /device:TPU:4, one launch (start us, length us, event | category | flops | bytes accessed | tf_op | source)
XLA Modules:
  0.0 369.7 jit_solution(14685394300023825922)
XLA Ops:
  8.3 14.9 %psum.21 = f32[2,16,4]{1,2,0:T(4,128)S(1)} all-reduce(f32[2,16,4]{1,2,0:T(4,128)S(1)} %pad_maximum_fusion.5), channel_id=1, replica_groups=mesh['z'=16,'x'=4,'narrow'=8] {'narrow'}, use_global_device_ids=true, to_apply=%region_2.0 | all-reduce | flops 128 | bytes 1024 | tf_op jit(solution)/shard_map/psum | solution.py:38
  27.0 23.9 %psum.22 = f32[16,4,160]{2,0,1:T(8,128)S(1)} all-reduce(f32[16,4,160]{2,0,1:T(8,128)S(1)} %fusion.180), channel_id=1, replica_groups=mesh['z'=16,'x'=4,'narrow'=8] {'narrow'}, use_global_device_ids=true, to_apply=%region_3.0 | all-reduce | flops 10240 | bytes 81920 | tf_op jit(solution)/shard_map/psum | solution.py:52
  52.2 23.6 %psum.23 = f32[16,4,64]{2,0,1:T(8,128)S(1)} all-reduce(f32[16,4,64]{2,0,1:T(8,128)S(1)} %fusion.98), channel_id=1, replica_groups=mesh['z'=16,'x'=4,'narrow'=8] {'narrow'}, use_global_device_ids=true, to_apply=%region_4.0 | all-reduce | flops 4096 | bytes 32768 | tf_op jit(solution)/shard_map/psum | solution.py:65
  76.0 14.7 %all_gather.9 = bf16[64,3328]{1,0:T(8,128)(2,1)} all-gather(bf16[16,3328]{1,0:T(8,128)(2,1)S(1)} %constant_dynamic-update-slice_fusion), channel_id=1, replica_groups=mesh['z'=16,'x'=4,'narrow'=8] {'x'}, dimensions={0}, use_global_device_ids=true | all-gather | bytes 532480 | tf_op jit(solution)/shard_map/all_gather | solution.py:75
  90.8 90.4 %all-gather.3.cloned.1.call-done = bf16[1024,3328]{1,0:T(8,128)(2,1)} async-done(((bf16[64,3328]{1,0:T(8,128)(2,1)}), bf16[1024,3328]{1,0:T(8,128)(2,1)}) %all-gather.3.cloned.1.call-update) | async-done | bytes 6815760 | tf_op jit(solution)/shard_map/all_gather | solution.py:74
  183.6 2.5 fusion.71
  186.1 2.5 fusion.73
  188.5 2.4 fusion.75
  191.0 2.5 fusion.77
  193.5 2.4 fusion.79
  195.9 2.4 fusion.81
  198.3 2.4 fusion.83
  200.7 2.4 fusion.85
  203.1 2.4 fusion.87
  205.6 2.4 fusion.89
  208.0 2.5 fusion.91
  210.5 2.4 fusion.61
  212.9 2.4 fusion.63
  217.7 2.4 fusion.67
  220.2 2.6 copy.62
  224.7 37.5 %reduce-scatter.4.cloned.1.call-done = bf16[128,1024]{1,0:T(8,128)(2,1)} async-done(((bf16[1024,1024]{1,0:T(8,128)(2,1)}), bf16[128,1024]{1,0:T(8,128)(2,1)}) %reduce-scatter.4.cloned.1.call-update) | async-done | bytes 262160
  272.3 8.7 %all_to_all.5 = bf16[4,64,512]{2,1,0:T(8,128)(2,1)} all-to-all(bf16[4,64,512]{2,1,0:T(8,128)(2,1)S(1)} %stack.27), channel_id=1, replica_groups=mesh['z'=16,'x'=4,'narrow'=8] {'x'}, dimensions={0} | all-to-all | bytes 524288 | tf_op jit(solution)/shard_map/all_to_all | solution.py:145
  281.0 78.3 %all-gather.5.cloned.1.call-done = bf16[4096,512]{1,0:T(8,128)(2,1)} async-done(((bf16[256,512]{1,0:T(8,128)(2,1)}), bf16[4096,512]{1,0:T(8,128)(2,1)}) %all-gather.5.cloned.1.call-update) | async-done | bytes 4194320 | tf_op jit(solution)/shard_map/all_gather | solution.py:144
  359.3 3.0 convolution_convert_fusion
  (88 shorter events, 23.8 us)
Async XLA Ops:
  7.2 352.1 %copy-start = (bf16[4096,64]{0,1:T(8,128)(2,1)S(1)}, bf16[4096,64]{0,1:T(8,128)(2,1)}, u32[]{:S(2)}) copy-start(bf16[4096,64]{0,1:T(8,128)(2,1)} %param.34) | copy-start | bytes 1572868
  7.2 174.0 %copy-start.5 = (bf16[5,32,512]{2,1,0:T(8,128)(2,1)S(1)}, bf16[5,32,512]{2,1,0:T(8,128)(2,1)}, u32[]{:S(2)}) copy-start(bf16[5,32,512]{2,1,0:T(8,128)(2,1)} %param.25) | copy-start | bytes 491524
  7.2 174.0 %copy-start.6 = (bf16[512,64]{0,1:T(8,128)(2,1)S(1)}, bf16[512,64]{0,1:T(8,128)(2,1)}, u32[]{:S(2)}) copy-start(bf16[512,64]{0,1:T(8,128)(2,1)} %param.30) | copy-start | bytes 196612
  7.2 174.0 %all-gather.3.cloned.1.call-start = ((), (), s32[]{:S(2)}) async-start(), calls=%async_computation.2 | async-start | bytes 7241728 | tf_op jit(solution)/shard_map/all_gather | solution.py:74
  90.7 92.9 %copy-start.7 = (bf16[512,64]{0,1:T(8,128)(2,1)S(1)}, bf16[512,64]{0,1:T(8,128)(2,1)}, u32[]{:S(2)}) copy-start(bf16[512,64]{0,1:T(8,128)(2,1)} %param.31) | copy-start | bytes 196612
  90.7 171.4 %reduce-scatter.4.cloned.1.call-start = ((), (), s32[]{:S(2)}) async-start(), calls=%async_computation.4 | async-start | bytes 2359296
  183.5 2.5 copy-start.8
  186.0 2.5 copy-start.9
  222.8 0.7 copy-start.2
  222.8 1.4 slice-start
  222.8 1.6 copy-start.10
  222.8 1.6 copy-start.11
  222.8 136.5 %all-gather.5.cloned.1.call-start = ((), (), s32[]{:S(2)}) async-start(), calls=%async_computation.3 | async-start | bytes 4456448 | tf_op jit(solution)/shard_map/all_gather | solution.py:144
  264.0 1.6 copy-start.1
  269.6 2.3 copy-start.3
  269.6 2.3 copy-start.4
Sparse Core Ops, SparseCore 0:
  90.8 90.2 all-gather.2
  222.9 39.2 reduce-scatter.3
  281.1 78.1 all-gather.4
